TPU v7x, 32 devices: a whole 2x2x4 slice. The times are simulated.
32 devices in a mesh: feat: 4 (over y, x), tok: 8 (over z, core).
Axes of the slice: x: 2, y: 2, z: 4, core: 2. Of those that a mesh axis runs over, the one named last changes fastest.
Arguments:
- tokens: bfloat16 [2048, 12288], P('tok', 'feat'), may hold values from -6 to 6
- gate_weight: bfloat16 [16, 5, 768, 768], P('feat', None, 'tok'), may hold values from -0.09375 to 0.09375
- up_weight: bfloat16 [16, 5, 768, 768], P('feat', None, 'tok'), may hold values from -0.09375 to 0.09375
- gate_scale: float32 [16, 5], P('feat'), may hold values from 0.35 to 2.8
- up_scale: float32 [16, 5], P('feat'), may hold values from 0.35 to 2.8
- partners: int32 [16, 5], replicated, may hold values from 0 to 15, as said below
- latent_in: bfloat16 [12288, 768], P('feat'), may hold values from -0.0546875 to 0.0546875
- latent_out: bfloat16 [768, 12288], P(None, 'feat'), may hold values from -0.21875 to 0.21875
Outputs:
- hidden: bfloat16 [2048, 12288], P('tok', 'feat')
- rank_term: bfloat16 [2048, 12288], P('tok', 'feat')
Inputs may be any that keep to these rules, and one draw needn't show every extreme that they name: `partners`: row i lists the blocks i, i xor 1, i xor 2, i xor 4 and i xor 8, each once, in some order.
All inputs are finite; a program needn't handle non-finite values.
Results may differ from a plain program's by a relative error of at most 0.015.
Values may be sent and summed in bfloat16 or wider, within the bound.
A program may use at most 128 MiB of HBM per device.

v0:
```python
import functools
import math

import jax
import jax.numpy as jnp
from jax import lax
from jax.experimental import pallas as pl
from jax.experimental.pallas import tpu as pltpu
from jax.sharding import PartitionSpec as P


PAIR = 2


def swapped(value, axis, bit):
    mask = 2**bit
    pairs = [(source, source ^ mask) for source in range(lax.axis_size(axis))]
    return lax.ppermute(value, axis, pairs)


def moved(value, chip_pairs):
    pairs = [
        (PAIR * source + lane, PAIR * target + lane)
        for source, target in chip_pairs
        for lane in range(PAIR)
    ]
    return lax.ppermute(value, "tok", pairs)


def join_kernel(slots, gate, up, gate_scale, up_scale, joined, *, block):
    slot = slots[block, pl.program_id(0)]
    width = gate.shape[-1]
    for start, weight, scale in ((0, gate, gate_scale), (width, up, up_scale)):
        product = weight[0, 0].astype(jnp.float32) * scale[block, slot]
        joined[0, :, start : start + width] = product.astype(joined.dtype)


def joined_weights(slots, gate_weight, up_weight, gate_scale, up_scale, block):
    _, slot_count, rows, width = gate_weight.shape
    picked = pl.BlockSpec((1, 1, rows, width), lambda k, slots: (block, slots[block, k], 0, 0))
    whole = pl.BlockSpec(memory_space=pltpu.SMEM)
    size = slot_count * rows * width
    return pl.pallas_call(
        lambda *refs: join_kernel(*refs, block=block),
        out_shape=jax.ShapeDtypeStruct((slot_count, rows, 2 * width), jnp.bfloat16),
        grid_spec=pltpu.PrefetchScalarGridSpec(
            num_scalar_prefetch=1,
            grid=(slot_count,),
            in_specs=[picked, picked, whole, whole],
            out_specs=pl.BlockSpec((1, rows, 2 * width), lambda k, slots: (k, 0, 0)),
        ),
        cost_estimate=pl.CostEstimate(flops=2 * size, bytes_accessed=8 * size, transcendentals=0),
    )(slots, gate_weight, up_weight, gate_scale, up_scale)


def part_blocks(blocks):
    return max(1, blocks // 2)


def per_device(
    tokens, gate_weight, up_weight, gate_scale, up_scale, partners, latent_in, latent_out
):
    tok_rows = tokens.shape[0]
    blocks, slot_count, part_rows, blk_width = gate_weight.shape
    feat_count = lax.axis_size("feat")
    chips = lax.axis_size("tok") // PAIR
    half = chips // 2
    local_bits = blocks.bit_length() - 1
    feat_bits = feat_count.bit_length() - 1
    place = lax.axis_index("tok")
    chip, lane = place // PAIR, place % PAIR
    on_right = chip >= half
    distance = jnp.where(on_right, chip - half, half - 1 - chip)
    inward = [[(half - 1 - q, half - 1), (half + q, half)] for q in range(half)]
    across = [[(half - 1 - q, half), (half + q, half - 1)] for q in range(half)]
    outward = [[(half - 1, half - 1 - q), (half, half + q)] for q in range(half)]

    first_block = lax.axis_index("feat") * blocks
    block_ids = first_block + jnp.arange(blocks, dtype=jnp.int32)
    offsets = [0] + [1 << bit_pos for bit_pos in range(local_bits + feat_bits)]
    labels = jnp.bitwise_xor(block_ids[:, None], jnp.array(offsets, dtype=jnp.int32)[None, :])
    wanted = lax.dynamic_slice_in_dim(partners, first_block, blocks, 0)
    matched = wanted[:, :, None] == labels[:, None, :]
    slot_ids = jnp.arange(slot_count, dtype=jnp.int32)
    slots = jnp.sum(jnp.where(matched, slot_ids[None, :, None], 0), axis=1)
    ready = [
        joined_weights(slots, gate_weight, up_weight, gate_scale, up_scale, own_block)
        for own_block in range(blocks)
    ]

    pieces = tokens.T.reshape(blocks, chips, PAIR, part_rows, tok_rows).transpose(2, 1, 0, 3, 4)
    pieces = jnp.where(lane == 0, pieces, pieces[::-1])
    left, right = pieces[:, :half][:, ::-1], pieces[:, half:]
    near = jnp.where(on_right, right, left)
    far = jnp.where(on_right, left, right)
    step = part_blocks(blocks)
    far_parts = [far[:, :, start : start + step] for start in range(0, blocks, step)]
    from_far = [[moved(part, across[q]) for part in far_parts] for q in range(half)]
    from_near = [[near]] + [[moved(near, inward[q])] for q in range(1, half)]
    shipped = [
        [ready[block]]
        + [moved(ready[block], inward[q]) for q in range(1, half)]
        for block in range(blocks)
    ]

    def turned(groups):
        return [
            [[swapped(value, "feat", bit) for value in parts] for bit in range(feat_bits)]
            for parts in groups
        ]

    far_remote = turned(from_far)
    near_remote = turned(from_near)

    def block_of(parts, block):
        size = blocks // len(parts)
        return parts[block // size][:, :, block % size]

    def inputs_of(own_block, groups, remotes):
        rows = []
        for group, remote in zip(groups, remotes):
            picked = [block_of(group, own_block)]
            for bit_pos in range(local_bits):
                picked.append(block_of(group, own_block ^ 1 << bit_pos))
            for bit_pos in range(feat_bits):
                picked.append(block_of(remote[bit_pos], own_block))
            rows.append(jnp.stack(picked, axis=2).reshape(-1, tok_rows))
        return jnp.concatenate(rows, axis=1)

    def product(inputs, weights):
        return lax.dot_general(
            inputs, weights, (((0,), (0,)), ((), ())), preferred_element_type=jnp.float32
        )

    latent_part = jnp.zeros((tok_rows, latent_in.shape[1]), jnp.float32)
    hidden = []
    for own_block in range(blocks):
        mine = jnp.concatenate(shipped[own_block], axis=0)
        other = swapped(mine, "tok", 0)
        weights = jnp.concatenate([mine, other], axis=0).reshape(-1, 2 * blk_width)
        inputs = inputs_of(own_block, from_far, far_remote)
        away = product(inputs, weights).astype(jnp.bfloat16)
        back = moved(away, across[0])
        inputs = inputs_of(own_block, from_near, near_remote)
        home = product(inputs, weights)
        sums = home + back.astype(jnp.float32)
        done = (jax.nn.silu(sums[:, :blk_width]) * sums[:, blk_width:]).astype(jnp.bfloat16)
        block_hidden = done[:tok_rows]
        for q in range(1, half):
            share = done[q * tok_rows : (q + 1) * tok_rows]
            sent = moved(share, outward[q])
            block_hidden = jnp.where(distance == q, sent, block_hidden)
        hidden.append(block_hidden)
        rows = latent_in[own_block * blk_width : (own_block + 1) * blk_width]
        latent_part += jnp.dot(block_hidden, rows, preferred_element_type=jnp.float32)
    latent = latent_part
    for bit_pos in range(feat_bits):
        share = latent.astype(jnp.bfloat16)
        latent = share.astype(jnp.float32) + swapped(share, "feat", bit_pos).astype(jnp.float32)
    latent = latent.astype(jnp.bfloat16)
    rank_term = jnp.dot(latent, latent_out, preferred_element_type=jnp.float32).astype(jnp.bfloat16)
    return (jnp.concatenate(hidden, axis=1), rank_term)


MESH = pl.DeviceIdType.MESH
VMEM_BYTES = 64 * 2**20
TILE = 256


def flipped(value, bit):
    mask = 2**bit
    return value + mask - 2 * mask * ((value // mask) % 2)


def hidden_kernel(
    half, feat_bits, partners, gate_scale, up_scale, tokens, gate, up, latent_in,
    hidden, latent, *scratch
):
    blocks, slot_count, part_rows, width = gate.shape
    rows = tokens.shape[0]
    parts = PAIR * half
    depth = parts * part_rows
    tile = math.gcd(width, TILE)
    cuts = width // tile
    steps = 2 * blocks * cuts
    pieces = blocks * cuts
    (
        weights, far_x, near_x, sent, got, early, made, factor, total, share, shared,
        far_out, far_land, near_out, near_land, near_own,
        turn_far_out, turn_far_land, turn_near_out, turn_near_land,
        weight_out, weight_land, lane_out, lane_land, weight_own,
        sum_out, sum_land, give_out, give_land, keep_own, factor_own, share_out, share_land,
    ) = scratch

    feat = lax.axis_index("feat")
    tok = lax.axis_index("tok")
    lane, chip = tok % PAIR, tok // PAIR
    side = chip // half
    distance = side * (chip - half) + (1 - side) * (half - 1 - chip)
    middle = (half - 1 + side) * PAIR + lane
    across = (half - side) * PAIR + lane
    partner = tok + 1 - 2 * lane

    def chip_of(which, q):
        return which * (half + q) + (1 - which) * (half - 1 - q)

    def tok_of(which, q):
        return chip_of(which, q) * PAIR + lane

    def part_of(q, which_lane):
        return (chip_of(side, q) - side * half) * PAIR + which_lane

    def remote(source, target, out, land, **where):
        return pltpu.make_async_remote_copy(
            src_ref=source,
            dst_ref=target,
            send_sem=out,
            recv_sem=land,
            device_id=where,
            device_id_type=MESH,
        )

    def columns(block, which):
        return pl.ds(pl.multiple_of(block * width + which * depth, math.gcd(width, depth)), depth)

    def far_copy(q, block, target):
        source = tokens.at[:, columns(block, 1 - side)]
        return remote(source, far_x.at[block, q], far_out.at[block], far_land.at[q, block], tok=target)

    def near_copy(q, block, target):
        source = tokens.at[:, columns(block, side)]
        return remote(source, near_x.at[block, q], near_out.at[block], near_land.at[q, block], tok=target)

    def turn_copy(x, q, block, bit, out, land):
        place = x.at[blocks * (1 + bit) + block, q]
        semaphores = out.at[bit, q, block], land.at[bit, q, block]
        return remote(x.at[block, q], place, *semaphores, feat=flipped(feat, bit))

    def stored(step):
        block, kind, cut = step // (2 * cuts), step // cuts % 2, step % cuts
        return (gate, up)[kind].at[block, :, :, pl.ds(cut * tile, tile)]

    def weight_copy(q, step, source, target):
        place = weights.at[step, :, part_of(q, lane)]
        return remote(source, place, weight_out.at[step], weight_land.at[q, step], tok=target)

    def lane_copy(q, step, source, which_lane):
        place = weights.at[step, :, part_of(q, which_lane)]
        source = place if source is None else source
        return remote(source, place, lane_out.at[q, step], lane_land.at[q, step], tok=partner)

    def own_copy(step, source):
        return pltpu.make_async_copy(
            source, weights.at[step, :, part_of(0, lane)], weight_own.at[step]
        )

    def sum_copy(q, step):
        return remote(sent.at[step, q], got.at[step, q], sum_out.at[q, step], sum_land.at[q, step], tok=across)

    def give_copy(q, piece, target):
        return remote(made.at[piece, q], made.at[piece, 0], give_out.at[q, piece], give_land.at[piece], tok=target)

    def keep_copy(piece):
        place = hidden.at[:, pl.ds(pl.multiple_of(piece * tile, tile), tile)]
        return pltpu.make_async_copy(made.at[piece, 0], place, keep_own.at[piece])

    def share_copy(stage, part):
        bit = (stage + part) % feat_bits
        semaphores = share_out.at[stage, part], share_land.at[stage, part]
        return remote(share.at[stage, part], shared.at[stage, part], *semaphores, feat=flipped(feat, bit))

    factor_copy = pltpu.make_async_copy(latent_in, factor, factor_own)
    factor_copy.start()
    barrier = pltpu.get_barrier_semaphore()

    def greet(peers):
        for peer in peers:
            pl.semaphore_signal(barrier, inc=1, device_id=peer, device_id_type=MESH)
        pl.semaphore_wait(barrier, len(peers))

    turns = [{"feat": flipped(feat, bit)} for bit in range(feat_bits)]

    def project(piece):
        total[...] += jnp.dot(
            made[piece, 0], factor[piece], preferred_element_type=jnp.float32
        )

    def clear():
        factor_copy.wait()
        total[...] = jnp.zeros_like(total)

    def near_after(block):
        return min(2 * cuts - 1 + 2 * block, steps - 1)

    first_home = max(near_after(blocks - 1) + 2, steps - 1 - (pieces - cuts))
    assert first_home < steps

    def outer(q):
        greet([{"tok": middle}, {"tok": across}] + turns)
        for step in range(cuts):
            weight_copy(q, step, stored(step), middle).start()
        for block in range(blocks):
            far_copy(q, block, across).start()
        for step in range(cuts, steps):
            weight_copy(q, step, stored(step), middle).start()
            for block in range(blocks):
                if near_after(block) == step:
                    near_copy(q, block, middle).start()
        clear()

        @pl.loop(0, pieces)
        def _(piece):
            give_copy(q, piece, middle).wait_recv()
            keep_copy(piece).start()
            project(piece)

        for block in range(blocks):
            far_copy(q, block, across).wait_send()
            near_copy(q, block, middle).wait_send()

        for step in range(steps):
            weight_copy(q, step, stored(step), middle).wait_send()

    def inner():
        peers = [{"tok": partner}, {"tok": across}]
        for q in range(1, half):
            peers += [{"tok": tok_of(which, q)} for which in (side, 1 - side)]
        greet(peers + turns)
        for block in range(blocks):
            far_copy(0, block, across).start()
        for step in range(steps):
            lane_copy(0, step, stored(step), lane).start()
            own_copy(step, stored(step)).start()
        near_own_copies = []
        for block in range(blocks):
            source = tokens.at[:, columns(block, side)]
            copy = pltpu.make_async_copy(source, near_x.at[block, 0], near_own.at[block])
            copy.start()
            near_own_copies.append(copy)

        far_turn = (turn_far_out, turn_far_land)
        near_turn = (turn_near_out, turn_near_land)

        def every_turn(x, semaphores, act):
            for block in range(blocks):
                for q in range(half):
                    for bit in range(feat_bits):
                        act(turn_copy(x, q, block, bit, *semaphores))

        for block in range(blocks):
            for q in range(half):
                far_copy(q, block, across).wait_recv()
                for bit in range(feat_bits):
                    turn_copy(far_x, q, block, bit, *far_turn).start()
        for block in range(blocks):
            near_own_copies[block].wait()
            for bit in range(feat_bits):
                turn_copy(near_x, 0, block, bit, *near_turn).start()
        clear()
        every_turn(far_x, far_turn, lambda copy: copy.wait_recv())

        def source_of(block, slot):
            row = feat * blocks + block
            label = partners[row, slot]
            place = label % blocks
            for bit in range(feat_bits):
                other = flipped(feat, bit) * blocks + block
                place = jnp.where(label == other, blocks * (1 + bit) + block, place)
            return place

        def sums(x, step):
            block, kind = step // (2 * cuts), step // cuts % 2
            value = None
            for slot in range(slot_count):
                scale = jnp.where(kind == 0, gate_scale[block, slot], up_scale[block, slot])
                inputs = x[source_of(block, slot)].reshape(half * rows, depth)
                weight = weights[step, slot].reshape(depth, tile)
                term = jnp.dot(inputs, weight, preferred_element_type=jnp.float32) * scale
                value = term if value is None else value + term
            return value

        def pair_of(piece):
            step = piece // cuts * 2 * cuts + piece % cuts
            return step, step + cuts

        def gated(first, second):
            return (first / (1.0 + jnp.exp(-first)) * second).astype(made.dtype)

        def home(piece):
            for q in range(half):
                for step in pair_of(piece):
                    sum_copy(q, step).wait_recv()
            first, second = [
                sums(near_x, step) + got[step].reshape(half * rows, tile).astype(jnp.float32)
                for step in pair_of(piece)
            ]
            made[piece] = gated(first, second).reshape(half, rows, tile)
            for q in range(1, half):
                give_copy(q, piece, tok_of(side, q)).start()
            keep_copy(piece).start()
            project(piece)

        @pl.loop(0, steps)
        def _(step):
            for q in range(1, half):
                weight_copy(q, step, stored(0), middle).wait_recv()
                lane_copy(q, step, None, lane).start()
            own_copy(step, stored(0)).wait()
            for q in range(half):
                lane_copy(q, step, None, 1 - lane).wait_recv()
            sent[step] = sums(far_x, step).astype(sent.dtype).reshape(half, rows, tile)
            for q in reversed(range(half)):
                sum_copy(q, step).start()
            for block in range(blocks):

                @pl.when(step == near_after(block))
                def _():
                    for q in range(1, half):
                        near_copy(q, block, middle).wait_recv()
                        for bit in range(feat_bits):
                            turn_copy(near_x, q, block, bit, *near_turn).start()

            @pl.when(step == first_home)
            def _():
                every_turn(near_x, near_turn, lambda copy: copy.wait_recv())

            @pl.when((step >= first_home) & (step < first_home + pieces - cuts))
            def _():
                home(step - first_home)

        @pl.loop(steps, first_home + pieces - cuts)
        def _(step):
            home(step - first_home)

        @pl.loop(0, cuts)
        def _(cut):
            for kind, step in enumerate(pair_of(pieces - cuts + cut)):
                early[kind, cut] = sums(near_x, step).reshape(half, rows, tile)

        @pl.loop(0, cuts)
        def _(cut):
            piece = pieces - cuts + cut
            for q in reversed(range(half)):
                values = []
                for kind, step in enumerate(pair_of(piece)):
                    sum_copy(q, step).wait_recv()
                    values.append(early[kind, cut, q] + got[step, q].astype(jnp.float32))
                made[piece, q] = gated(*values)
                if q:
                    give_copy(q, piece, tok_of(side, q)).start()
            keep_copy(piece).start()
            project(piece)

    for q in range(1, half):
        pl.when(distance == q)(lambda q=q: outer(q))
    pl.when(distance == 0)(inner)

    part_width = total.shape[1] // feat_bits
    for stage in range(feat_bits):
        for part in range(feat_bits):
            span = pl.ds(part * part_width, part_width)
            share[stage, part] = total[:, span].astype(share.dtype)
            share_copy(stage, part).start()
        for part in range(feat_bits):
            span = pl.ds(part * part_width, part_width)
            share_copy(stage, part).wait_recv()
            ours = share[stage, part].astype(jnp.float32)
            total[:, span] = ours + shared[stage, part].astype(jnp.float32)
    latent[...] = total[...].astype(latent.dtype)

    @pl.loop(0, pieces)
    def _(piece):
        keep_copy(piece).wait()

    for stage in range(feat_bits):
        for part in range(feat_bits):
            share_copy(stage, part).wait_send()

    @pl.when(distance == 0)
    def _():
        for block in range(blocks):
            far_copy(0, block, across).wait_send()
            for q in range(half):
                for bit in range(feat_bits):
                    turn_copy(far_x, q, block, bit, turn_far_out, turn_far_land).wait_send()
                    turn_copy(near_x, q, block, bit, turn_near_out, turn_near_land).wait_send()

        @pl.loop(0, steps)
        def _(step):
            for q in range(half):
                lane_copy(q, step, None, lane).wait_send()
                sum_copy(q, step).wait_send()

        @pl.loop(0, pieces)
        def _(piece):
            for q in range(1, half):
                give_copy(q, piece, tok_of(side, q)).wait_send()


def kernel_scratch(half, feat_bits, rows, weight_shape, rank):
    blocks, slot_count, part_rows, width = weight_shape
    tile = math.gcd(width, TILE)
    cuts = width // tile
    steps, pieces = 2 * blocks * cuts, blocks * cuts
    parts = PAIR * half
    sources = blocks * (1 + feat_bits)
    depth = parts * part_rows
    low, high = jnp.bfloat16, jnp.float32
    arrays = [
        ((steps, slot_count, parts, part_rows, tile), low),
        ((sources, half, rows, depth), low),
        ((sources, half, rows, depth), low),
        ((steps, half, rows, tile), low),
        ((steps, half, rows, tile), low),
        ((2, cuts, half, rows, tile), high),
        ((pieces, half, rows, tile), low),
        ((pieces, tile, rank), low),
        ((rows, rank), high),
        ((feat_bits, feat_bits, rows, rank // feat_bits), low),
        ((feat_bits, feat_bits, rows, rank // feat_bits), low),
    ]
    turns = (feat_bits, half, blocks)
    counts = [
        (blocks,), (half, blocks), (blocks,), (half, blocks), (blocks,),
        turns, turns, turns, turns,
        (steps,), (half, steps), (half, steps), (half, steps), (steps,),
        (half, steps), (half, steps), (half, pieces), (pieces,), (pieces,), (),
        (feat_bits, feat_bits), (feat_bits, feat_bits),
    ]
    return arrays, counts


def kernel_fits(half, feat_bits, rows, weight_shape, rank):
    arrays, _ = kernel_scratch(half, feat_bits, rows, weight_shape, rank)
    size = sum(math.prod(shape) * jnp.dtype(kind).itemsize for shape, kind in arrays)
    return half > 1 and size <= VMEM_BYTES * 15 // 16


def hidden_of(tokens, gate_weight, up_weight, gate_scale, up_scale, partners, latent_in):
    half = lax.axis_size("tok") // PAIR // 2
    feat_bits = lax.axis_size("feat").bit_length() - 1
    rows, rank = tokens.shape[0], latent_in.shape[1]
    arrays, counts = kernel_scratch(half, feat_bits, rows, gate_weight.shape, rank)
    factor = latent_in.reshape(-1, math.gcd(gate_weight.shape[3], TILE), rank)
    scalars = pl.BlockSpec(memory_space=pltpu.SMEM)
    whole = pl.BlockSpec(memory_space=pl.ANY)
    return pl.pallas_call(
        functools.partial(hidden_kernel, half, feat_bits),
        out_shape=(
            jax.ShapeDtypeStruct(tokens.shape, jnp.bfloat16),
            jax.ShapeDtypeStruct((rows, rank), jnp.bfloat16),
        ),
        in_specs=[scalars] * 3 + [whole] * 4,
        out_specs=(whole, pl.BlockSpec(memory_space=pltpu.VMEM)),
        scratch_shapes=[pltpu.VMEM(*one) for one in arrays]
        + [pltpu.SemaphoreType.DMA(count) for count in counts],
        compiler_params=pltpu.CompilerParams(
            collective_id=0, has_side_effects=True, vmem_limit_bytes=VMEM_BYTES - 2**17
        ),
        name="hidden",
    )(partners, gate_scale, up_scale, tokens, gate_weight, up_weight, factor)


def fused(tokens, gate_weight, up_weight, gate_scale, up_scale, partners, latent_in, latent_out):
    hidden, latent = hidden_of(
        tokens, gate_weight, up_weight, gate_scale, up_scale, partners, latent_in
    )
    rank_term = jnp.dot(latent, latent_out, preferred_element_type=jnp.float32).astype(jnp.bfloat16)
    return hidden, rank_term


def solution(mesh):
    placed = (
        P("tok", "feat"),
        P("feat", None, "tok", None),
        P("feat", None, "tok", None),
        P("feat", None),
        P("feat", None),
        P(),
        P("feat", None),
        P(None, "feat"),
    )
    feat_bits = mesh.shape["feat"].bit_length() - 1
    half = mesh.shape["tok"] // PAIR // 2

    def sharded(function):
        return jax.shard_map(
            function,
            mesh=mesh,
            in_specs=placed,
            out_specs=(P("tok", "feat"), P("tok", "feat")),
            check_vma=False,
        )

    def run(*args):
        rows = args[0].shape[0] // mesh.shape["tok"]
        blocks, slot_count, depth, width = args[1].shape
        blocks //= mesh.shape["feat"]
        local = (blocks, slot_count, depth // mesh.shape["tok"], width)
        if kernel_fits(half, feat_bits, rows, local, args[6].shape[1]):
            return sharded(fused)(*args)
        return sharded(per_device)(*args)

    return run
```

profile of v0, /device:TPU:0, one launch (start us, length us, event | category | flops | bytes accessed | tf_op | source)
XLA Modules:
  0.0 226.2 jit_solution(4530656725990681984)
XLA Ops:
  0.6 1.4 copy.10.partners
  2.0 217.9 %hidden.1 = (bf16[256,3072]{1,0:T(8,128)(2,1)}, bf16[256,768]{1,0:T(8,128)(2,1)}) custom-call(s32[16,5]{1,0:T(8,128)} %copy.10.partners, f32[4,5]{1,0:T(4,128)} %gate_scale.1, f32[4,5]{1,0:T(4,128)} %up_scale.1, bf16[256,3072]{1,0:T(8,128)(2,1)} %tokens.1, bf16[4,5,96,768]{3,2,1,0:T(8,128)(2,1)} %gate.1, bf16[4,5,96,768]{3,2,1,0:T(8,128)(2,1)} %up.1, ...), custom_call_target="tpu_custom_call" | custom-call | tf_op jit(solution)/shard_map/hidden/pallas_call | solution.py:547
  219.9 0.0 copy-start
  220.0 5.1 %convolution_convert_fusion = bf16[256,3072]{1,0:T(8,128)(2,1)} fusion(bf16[256,768]{1,0:T(8,128)(2,1)} %get-tuple-element.5, bf16[768,3072]{1,0:T(8,128)(2,1)} %param.15), kind=kOutput, calls=%fused_computation | convolution fusion | flops 1208745984 | bytes 6684672 | tf_op jit(solution)/shard_map/dot_general | solution.py:568
  225.1 0.0 copy-done
  225.1 1.1 copy.12
Async XLA Ops:
  219.9 5.1 %copy-start = (bf16[256,3072]{1,0:T(8,128)(2,1)S(1)}, bf16[256,3072]{1,0:T(8,128)(2,1)}, u32[]{:S(2)}) copy-start(bf16[256,3072]{1,0:T(8,128)(2,1)} %get-tuple-element.8) | copy-start | bytes 4718596
where the time goes:
time: 226 us
  Pallas kernels  218 us (96%)
  matrix products  5.11 us (2%)
  local copies, waits for them, and re-layouts  2.51 us (1%)
    pallas_call x1, Pallas kernels, hidden_of(): pl.pallas_call(functools.partial(hidden_kernel, half, feat_bits), out_sha...  218 us
    dot_general x1, matrix products, fused(): jnp.dot(latent, latent_out, preferred_element_type=jnp.float32)  5.11 us

commit v1 on v0

--- a/solution.py
+++ b/solution.py
@@ -165,6 +165,8 @@
 MESH = pl.DeviceIdType.MESH
 VMEM_BYTES = 64 * 2**20
 TILE = 256
+RING = 6
+SPARE_BYTES = 3 * 2**20
 
 
 def flipped(value, bit):
@@ -184,13 +186,16 @@
     cuts = width // tile
     steps = 2 * blocks * cuts
     pieces = blocks * cuts
+    far_x, scratch = scratch[:half], scratch[half:]
     (
-        weights, far_x, near_x, sent, got, early, made, factor, total, share, shared,
+        weights, near_x, sent, got, ready, made, factor, total, share, shared, wanted,
         far_out, far_land, near_out, near_land, near_own,
         turn_far_out, turn_far_land, turn_near_out, turn_near_land,
         weight_out, weight_land, lane_out, lane_land, weight_own,
         sum_out, sum_land, give_out, give_land, keep_own, factor_own, share_out, share_land,
+        wanted_own,
     ) = scratch
+    ring = sent.shape[0]
 
     feat = lax.axis_index("feat")
     tok = lax.axis_index("tok")
@@ -225,16 +230,24 @@
 
     def far_copy(q, block, target):
         source = tokens.at[:, columns(block, 1 - side)]
-        return remote(source, far_x.at[block, q], far_out.at[block], far_land.at[q, block], tok=target)
+        return remote(source, far_x[q].at[block], far_out, far_land.at[q, block], tok=target)
 
     def near_copy(q, block, target):
         source = tokens.at[:, columns(block, side)]
-        return remote(source, near_x.at[block, q], near_out.at[block], near_land.at[q, block], tok=target)
-
-    def turn_copy(x, q, block, bit, out, land):
-        place = x.at[blocks * (1 + bit) + block, q]
-        semaphores = out.at[bit, q, block], land.at[bit, q, block]
-        return remote(x.at[block, q], place, *semaphores, feat=flipped(feat, bit))
+        return remote(source, near_x.at[block, q], near_out, near_land.at[q, block], tok=target)
+
+    def far_turn(q, block, bit):
+        source, place = [far_x[q].at[at] for at in (block, blocks * (1 + bit) + block)]
+        semaphores = turn_far_out.at[q], turn_far_land.at[bit, q, block]
+        return remote(source, place, *semaphores, feat=flipped(feat, bit))
+
+    def near_turn(q, block, bit):
+        source, place = [near_x.at[at, q] for at in (block, blocks * (1 + bit) + block)]
+        semaphores = turn_near_out, turn_near_land.at[bit, q, block]
+        return remote(source, place, *semaphores, feat=flipped(feat, bit))
+
+    def settle(whole, semaphore):
+        pltpu.make_async_copy(whole, whole, semaphore).wait()
 
     def stored(step):
         block, kind, cut = step // (2 * cuts), step // cuts % 2, step % cuts
@@ -242,35 +255,38 @@
 
     def weight_copy(q, step, source, target):
         place = weights.at[step, :, part_of(q, lane)]
-        return remote(source, place, weight_out.at[step], weight_land.at[q, step], tok=target)
+        return remote(source, place, weight_out, weight_land.at[q, step], tok=target)
 
     def lane_copy(q, step, source, which_lane):
         place = weights.at[step, :, part_of(q, which_lane)]
         source = place if source is None else source
-        return remote(source, place, lane_out.at[q, step], lane_land.at[q, step], tok=partner)
+        return remote(source, place, lane_out, lane_land.at[step], tok=partner)
 
     def own_copy(step, source):
         return pltpu.make_async_copy(
-            source, weights.at[step, :, part_of(0, lane)], weight_own.at[step]
+            source, weights.at[step, :, part_of(0, lane)], weight_own
         )
 
     def sum_copy(q, step):
-        return remote(sent.at[step, q], got.at[step, q], sum_out.at[q, step], sum_land.at[q, step], tok=across)
+        slot = step % ring
+        return remote(sent.at[slot, q], got.at[step, q], sum_out.at[slot], sum_land.at[q, step], tok=across)
 
     def give_copy(q, piece, target):
-        return remote(made.at[piece, q], made.at[piece, 0], give_out.at[q, piece], give_land.at[piece], tok=target)
+        return remote(made.at[piece, q], made.at[piece, 0], give_out, give_land.at[piece], tok=target)
 
     def keep_copy(piece):
         place = hidden.at[:, pl.ds(pl.multiple_of(piece * tile, tile), tile)]
-        return pltpu.make_async_copy(made.at[piece, 0], place, keep_own.at[piece])
+        return pltpu.make_async_copy(made.at[piece, 0], place, keep_own)
 
     def share_copy(stage, part):
         bit = (stage + part) % feat_bits
-        semaphores = share_out.at[stage, part], share_land.at[stage, part]
+        semaphores = share_out, share_land.at[stage, part]
         return remote(share.at[stage, part], shared.at[stage, part], *semaphores, feat=flipped(feat, bit))
 
     factor_copy = pltpu.make_async_copy(latent_in, factor, factor_own)
     factor_copy.start()
+    wanted_copy = pltpu.make_async_copy(partners, wanted, wanted_own)
+    wanted_copy.start()
     barrier = pltpu.get_barrier_semaphore()
 
     def greet(peers):
@@ -287,21 +303,23 @@
 
     def clear():
         factor_copy.wait()
+        wanted_copy.wait()
         total[...] = jnp.zeros_like(total)
 
     def near_after(block):
         return min(2 * cuts - 1 + 2 * block, steps - 1)
 
+    early_steps = max(1, cuts - 1)
     first_home = max(near_after(blocks - 1) + 2, steps - 1 - (pieces - cuts))
     assert first_home < steps
 
     def outer(q):
         greet([{"tok": middle}, {"tok": across}] + turns)
-        for step in range(cuts):
+        for step in range(early_steps):
             weight_copy(q, step, stored(step), middle).start()
         for block in range(blocks):
             far_copy(q, block, across).start()
-        for step in range(cuts, steps):
+        for step in range(early_steps, steps):
             weight_copy(q, step, stored(step), middle).start()
             for block in range(blocks):
                 if near_after(block) == step:
@@ -314,12 +332,9 @@
             keep_copy(piece).start()
             project(piece)
 
-        for block in range(blocks):
-            far_copy(q, block, across).wait_send()
-            near_copy(q, block, middle).wait_send()
-
-        for step in range(steps):
-            weight_copy(q, step, stored(step), middle).wait_send()
+        settle(far_x[0].at[pl.ds(0, blocks)], far_out)
+        settle(near_x.at[pl.ds(0, blocks), 0], near_out)
+        settle(weights.at[:, :, 0], weight_out)
 
     def inner():
         peers = [{"tok": partner}, {"tok": across}]
@@ -331,53 +346,53 @@
         for step in range(steps):
             lane_copy(0, step, stored(step), lane).start()
             own_copy(step, stored(step)).start()
-        near_own_copies = []
         for block in range(blocks):
             source = tokens.at[:, columns(block, side)]
-            copy = pltpu.make_async_copy(source, near_x.at[block, 0], near_own.at[block])
-            copy.start()
-            near_own_copies.append(copy)
-
-        far_turn = (turn_far_out, turn_far_land)
-        near_turn = (turn_near_out, turn_near_land)
-
-        def every_turn(x, semaphores, act):
+            pltpu.make_async_copy(source, near_x.at[block, 0], near_own).start()
+
+        def take_far(q, block):
+            far_copy(q, block, across).wait_recv()
+            for bit in range(feat_bits):
+                far_turn(q, block, bit).start()
+
+        def turned_far(q):
             for block in range(blocks):
-                for q in range(half):
-                    for bit in range(feat_bits):
-                        act(turn_copy(x, q, block, bit, *semaphores))
-
-        for block in range(blocks):
-            for q in range(half):
-                far_copy(q, block, across).wait_recv()
                 for bit in range(feat_bits):
-                    turn_copy(far_x, q, block, bit, *far_turn).start()
-        for block in range(blocks):
-            near_own_copies[block].wait()
-            for bit in range(feat_bits):
-                turn_copy(near_x, 0, block, bit, *near_turn).start()
-        clear()
-        every_turn(far_x, far_turn, lambda copy: copy.wait_recv())
+                    far_turn(q, block, bit).wait_recv()
 
         def source_of(block, slot):
             row = feat * blocks + block
-            label = partners[row, slot]
+            label = wanted[slot, row]
             place = label % blocks
             for bit in range(feat_bits):
                 other = flipped(feat, bit) * blocks + block
                 place = jnp.where(label == other, blocks * (1 + bit) + block, place)
             return place
 
-        def sums(x, step):
+        def sums(step, load):
             block, kind = step // (2 * cuts), step // cuts % 2
             value = None
             for slot in range(slot_count):
                 scale = jnp.where(kind == 0, gate_scale[block, slot], up_scale[block, slot])
-                inputs = x[source_of(block, slot)].reshape(half * rows, depth)
+                inputs = load(source_of(block, slot))
                 weight = weights[step, slot].reshape(depth, tile)
                 term = jnp.dot(inputs, weight, preferred_element_type=jnp.float32) * scale
                 value = term if value is None else value + term
             return value
+
+        def near_sums(step):
+            return sums(step, lambda at: near_x[at].reshape(half * rows, depth))
+
+        def far_sums(step):
+            return sums(step, lambda at: jnp.concatenate([x[at] for x in far_x], axis=0))
+
+        def part_sums(q, step):
+            return sums(step, lambda at: far_x[q][at])
+
+        def pass_on(step):
+            for q in range(1, half):
+                weight_copy(q, step, stored(0), middle).wait_recv()
+                lane_copy(q, step, None, lane).start()
 
         def pair_of(piece):
             step = piece // cuts * 2 * cuts + piece % cuts
@@ -391,7 +406,7 @@
                 for step in pair_of(piece):
                     sum_copy(q, step).wait_recv()
             first, second = [
-                sums(near_x, step) + got[step].reshape(half * rows, tile).astype(jnp.float32)
+                near_sums(step) + got[step].reshape(half * rows, tile).astype(jnp.float32)
                 for step in pair_of(piece)
             ]
             made[piece] = gated(first, second).reshape(half, rows, tile)
@@ -400,15 +415,45 @@
             keep_copy(piece).start()
             project(piece)
 
-        @pl.loop(0, steps)
+        def early(q):
+            @pl.loop(0, early_steps)
+            def _(step):
+                sent[step, q] = part_sums(q, step).astype(sent.dtype)
+                sum_copy(q, step).start()
+
+        for block in range(blocks):
+            take_far(0, block)
+        for step in range(early_steps):
+            pass_on(step)
+        clear()
+        settle(weights.at[:, :, 0], weight_own)
+        for q in range(1, half):
+            take_far(q, 0)
+        for step in range(early_steps):
+            settle(weights.at[step, :, pl.ds(0, half)], lane_land.at[step])
+        turned_far(0)
+        early(0)
+        for block in range(1, blocks):
+            for q in range(1, half):
+                take_far(q, block)
+        settle(near_x.at[pl.ds(0, blocks), 0], near_own)
+        for block in range(blocks):
+            for bit in range(feat_bits):
+                near_turn(0, block, bit).start()
+        for q in range(1, half):
+            turned_far(q)
+            early(q)
+
+        @pl.loop(early_steps, steps)
         def _(step):
-            for q in range(1, half):
-                weight_copy(q, step, stored(0), middle).wait_recv()
-                lane_copy(q, step, None, lane).start()
-            own_copy(step, stored(0)).wait()
-            for q in range(half):
-                lane_copy(q, step, None, 1 - lane).wait_recv()
-            sent[step] = sums(far_x, step).astype(sent.dtype).reshape(half, rows, tile)
+            pass_on(step)
+            settle(weights.at[step, :, pl.ds(0, half)], lane_land.at[step])
+
+            @pl.when(step >= ring)
+            def _():
+                settle(sent.at[step % ring], sum_out.at[step % ring])
+
+            sent[step % ring] = far_sums(step).astype(sent.dtype).reshape(half, rows, tile)
             for q in reversed(range(half)):
                 sum_copy(q, step).start()
             for block in range(blocks):
@@ -418,11 +463,14 @@
                     for q in range(1, half):
                         near_copy(q, block, middle).wait_recv()
                         for bit in range(feat_bits):
-                            turn_copy(near_x, q, block, bit, *near_turn).start()
+                            near_turn(q, block, bit).start()
 
             @pl.when(step == first_home)
             def _():
-                every_turn(near_x, near_turn, lambda copy: copy.wait_recv())
+                for block in range(blocks):
+                    for q in range(half):
+                        for bit in range(feat_bits):
+                            near_turn(q, block, bit).wait_recv()
 
             @pl.when((step >= first_home) & (step < first_home + pieces - cuts))
             def _():
@@ -435,7 +483,7 @@
         @pl.loop(0, cuts)
         def _(cut):
             for kind, step in enumerate(pair_of(pieces - cuts + cut)):
-                early[kind, cut] = sums(near_x, step).reshape(half, rows, tile)
+                ready[kind, cut] = near_sums(step).reshape(half, rows, tile)
 
         @pl.loop(0, cuts)
         def _(cut):
@@ -444,7 +492,7 @@
                 values = []
                 for kind, step in enumerate(pair_of(piece)):
                     sum_copy(q, step).wait_recv()
-                    values.append(early[kind, cut, q] + got[step, q].astype(jnp.float32))
+                    values.append(ready[kind, cut, q] + got[step, q].astype(jnp.float32))
                 made[piece, q] = gated(*values)
                 if q:
                     give_copy(q, piece, tok_of(side, q)).start()
@@ -468,33 +516,19 @@
             total[:, span] = ours + shared[stage, part].astype(jnp.float32)
     latent[...] = total[...].astype(latent.dtype)
 
-    @pl.loop(0, pieces)
-    def _(piece):
-        keep_copy(piece).wait()
-
-    for stage in range(feat_bits):
-        for part in range(feat_bits):
-            share_copy(stage, part).wait_send()
+    settle(made.at[:, 0], keep_own)
+    settle(share, share_out)
 
     @pl.when(distance == 0)
     def _():
-        for block in range(blocks):
-            far_copy(0, block, across).wait_send()
-            for q in range(half):
-                for bit in range(feat_bits):
-                    turn_copy(far_x, q, block, bit, turn_far_out, turn_far_land).wait_send()
-                    turn_copy(near_x, q, block, bit, turn_near_out, turn_near_land).wait_send()
-
-        @pl.loop(0, steps)
-        def _(step):
-            for q in range(half):
-                lane_copy(q, step, None, lane).wait_send()
-                sum_copy(q, step).wait_send()
-
-        @pl.loop(0, pieces)
-        def _(piece):
-            for q in range(1, half):
-                give_copy(q, piece, tok_of(side, q)).wait_send()
+        settle(far_x[0].at[pl.ds(0, blocks)], far_out)
+        for q in range(half):
+            settle(far_x[q].at[pl.ds(blocks, blocks * feat_bits)], turn_far_out.at[q])
+        settle(near_x.at[pl.ds(blocks, blocks * feat_bits)], turn_near_out)
+        settle(weights.at[:, :, pl.ds(0, half)], lane_out)
+        for slot in range(ring):
+            settle(sent.at[slot], sum_out.at[slot])
+        settle(made.at[:, pl.ds(1, half - 1)], give_out)
 
 
 def kernel_scratch(half, feat_bits, rows, weight_shape, rank):
@@ -506,11 +540,11 @@
     sources = blocks * (1 + feat_bits)
     depth = parts * part_rows
     low, high = jnp.bfloat16, jnp.float32
-    arrays = [
+    arrays = [((sources, rows, depth), low)] * half
+    arrays += [
         ((steps, slot_count, parts, part_rows, tile), low),
         ((sources, half, rows, depth), low),
-        ((sources, half, rows, depth), low),
-        ((steps, half, rows, tile), low),
+        ((min(RING, steps), half, rows, tile), low),
         ((steps, half, rows, tile), low),
         ((2, cuts, half, rows, tile), high),
         ((pieces, half, rows, tile), low),
@@ -521,19 +555,22 @@
     ]
     turns = (feat_bits, half, blocks)
     counts = [
-        (blocks,), (half, blocks), (blocks,), (half, blocks), (blocks,),
-        turns, turns, turns, turns,
-        (steps,), (half, steps), (half, steps), (half, steps), (steps,),
-        (half, steps), (half, steps), (half, pieces), (pieces,), (pieces,), (),
-        (feat_bits, feat_bits), (feat_bits, feat_bits),
+        (), (half, blocks), (), (half, blocks), (),
+        (half,), turns, (), turns,
+        (), (half, steps), (), (steps,), (),
+        (min(RING, steps),), (half, steps), (), (pieces,), (), (),
+        (), (feat_bits, feat_bits), (),
     ]
     return arrays, counts
 
 
+def kernel_bytes(arrays):
+    return sum(math.prod(shape) * jnp.dtype(kind).itemsize for shape, kind in arrays)
+
+
 def kernel_fits(half, feat_bits, rows, weight_shape, rank):
     arrays, _ = kernel_scratch(half, feat_bits, rows, weight_shape, rank)
-    size = sum(math.prod(shape) * jnp.dtype(kind).itemsize for shape, kind in arrays)
-    return half > 1 and size <= VMEM_BYTES * 15 // 16
+    return half > 1 and kernel_bytes(arrays) <= VMEM_BYTES * 7 // 8
 
 
 def hidden_of(tokens, gate_weight, up_weight, gate_scale, up_scale, partners, latent_in):
@@ -550,15 +587,16 @@
             jax.ShapeDtypeStruct(tokens.shape, jnp.bfloat16),
             jax.ShapeDtypeStruct((rows, rank), jnp.bfloat16),
         ),
-        in_specs=[scalars] * 3 + [whole] * 4,
+        in_specs=[whole] + [scalars] * 2 + [whole] * 4,
         out_specs=(whole, pl.BlockSpec(memory_space=pltpu.VMEM)),
         scratch_shapes=[pltpu.VMEM(*one) for one in arrays]
+        + [pltpu.SMEM(partners.shape[::-1], partners.dtype)]
         + [pltpu.SemaphoreType.DMA(count) for count in counts],
         compiler_params=pltpu.CompilerParams(
-            collective_id=0, has_side_effects=True, vmem_limit_bytes=VMEM_BYTES - 2**17
+            collective_id=0, has_side_effects=True, vmem_limit_bytes=kernel_bytes(arrays) + SPARE_BYTES
         ),
         name="hidden",
-    )(partners, gate_scale, up_scale, tokens, gate_weight, up_weight, factor)
+    )(partners.T, gate_scale, up_scale, tokens, gate_weight, up_weight, factor)
 
 
 def fused(tokens, gate_weight, up_weight, gate_scale, up_scale, partners, latent_in, latent_out):

time: 226 us -> 216 us (0.956)
  Pallas kernels: 218 us -> 210 us
    pallas_call x1, Pallas kernels: 218 us -> 210 us  [hidden_of(): pl.pallas_call(functools.partial(hidden_kernel, half, feat_bits), out_sha...]
where the time goes in v1:
time: 216 us
  Pallas kernels  210 us (97%)
  matrix products  3.65 us (2%)
    pallas_call x1, Pallas kernels, hidden_of(): pl.pallas_call(functools.partial(hidden_kernel, half, feat_bits), out_sha...  210 us

profile of v1, /device:TPU:0, one launch (start us, length us, event | category | flops | bytes accessed | tf_op | source)
XLA Modules:
  0.0 215.8 jit_solution(11713855085623955551)
XLA Ops:
  0.6 0.0 copy-start.1
  0.6 210.3 %hidden.1 = (bf16[256,3072]{1,0:T(8,128)(2,1)}, bf16[256,768]{1,0:T(8,128)(2,1)}) custom-call(s32[5,16]{1,0:T(8,128)} %bitcast.5, f32[4,5]{1,0:T(4,128)} %gate_scale.1, f32[4,5]{1,0:T(4,128)} %up_scale.1, bf16[256,3072]{1,0:T(8,128)(2,1)} %tokens.1, bf16[4,5,96,768]{3,2,1,0:T(8,128)(2,1)} %gate.1, bf16[4,5,96,768]{3,2,1,0:T(8,128)(2,1)} %up.1, ...), custom_call_target="tpu_custom_call" | custom-call | tf_op jit(solution)/shard_map/hidden/pallas_call | solution.py:584
  211.0 0.0 copy-done.1
  211.0 0.0 copy-start
  211.0 3.6 %convolution_convert_fusion = bf16[256,3072]{1,0:T(8,128)(2,1)} fusion(bf16[256,768]{1,0:T(8,128)(2,1)} %get-tuple-element.5, bf16[768,3072]{1,0:T(8,128)(2,1)S(1)} %copy-done.1), kind=kOutput, calls=%fused_computation | convolution fusion | flops 1208745984 | bytes 6684672 | tf_op jit(solution)/shard_map/dot_general | solution.py:606
  214.7 0.0 copy-done
  214.7 1.1 copy.11
Async XLA Ops:
  0.6 210.4 %copy-start.1 = (bf16[768,3072]{1,0:T(8,128)(2,1)S(1)}, bf16[768,3072]{1,0:T(8,128)(2,1)}, u32[]{:S(2)}) copy-start(bf16[768,3072]{1,0:T(8,128)(2,1)} %param.15) | copy-start | bytes 14155780
  211.0 3.7 %copy-start = (bf16[256,3072]{1,0:T(8,128)(2,1)S(1)}, bf16[256,3072]{1,0:T(8,128)(2,1)}, u32[]{:S(2)}) copy-start(bf16[256,3072]{1,0:T(8,128)(2,1)} %get-tuple-element.8) | copy-start | bytes 4718596
